TPU v7x, 256 devices: a whole 4x4x8 slice. The times are simulated.
256 devices in a mesh: ex: 16 (over y_hi, x, core), co: 16 (over y_lo, z).
Axes of the slice: x: 4, y: 4 (y_hi: 2, y_lo: 2; y = y_hi * 2 + y_lo), z: 8, core: 2. Of those that a mesh axis runs over, the one named last changes fastest.
Arguments:
- train_grads: float32 [16384, 32768], P('ex', 'co')
- queries: float32 [1024, 32768], P('ex', 'co'), may hold values from -6 to 6
- module_ids: int32 [8], replicated, may hold values from 0 to 223
- module_scale: float32 [224], replicated, may hold values from 0.3 to 3
- example_ids: int32 [16384], P('ex'), may hold values from 0 to 16383, as said below
Outputs:
- influence: float32 [1024, 16384], P('co', 'ex')
Inputs may be any that keep to these rules, and one draw needn't show every extreme that they name: `example_ids`: the examples of block s of 1024 rows carry the ids s * 1024 to (s + 1) * 1024 - 1, each once.
All inputs are finite; a program needn't handle non-finite values.
Results may differ from a plain program's by a relative error of at most 0.00008.
Values sent between devices are 32-bit elements; how exact they have to be, the bound alone decides.
No kernel may reach another device: no remote copies, remote signals or barrier semaphores. Data moves between devices by JAX's collectives and lax.ppermute only.
A program may use at most 128 MiB of HBM per device.

v0:
```python
import jax
import jax.numpy as jnp
from jax import lax
from jax.sharding import PartitionSpec as P

PROJ = 4096
epsilon = 1e-06


def total_of_pieces(x, axis):
    return lax.all_gather(x, axis).sum(0)


def score_block(query_rows, train_grads):
    return lax.dot_general(
        query_rows,
        train_grads,
        (((1,), (1,)), ((), ())),
        precision=lax.Precision.HIGHEST,
        preferred_element_type=jnp.float32,
    )


def shards(train_grads, queries, module_ids, module_scale, example_ids):
    example_count = train_grads.shape[0]
    coord_count = train_grads.shape[1]
    module_count = module_ids.shape[0]
    offset = lax.axis_index("co") * coord_count
    position = offset + lax.iota(jnp.int32, coord_count)
    table_index = lax.iota(jnp.int32, module_scale.shape[0])
    picked = jnp.sum(
        jnp.where(module_ids[:, None] == table_index[None, :], module_scale[None, :], 0.0), axis=1
    )
    window_index = lax.iota(jnp.int32, module_count)
    local_module = position // PROJ
    coord_scale = jnp.sum(
        jnp.where(local_module[:, None] == window_index[None, :], picked[None, :], 0.0), axis=1
    )
    scaled = queries * coord_scale[None, :]
    squares = jnp.sum(train_grads * train_grads, axis=1)
    norm_total = total_of_pieces(squares, "co")
    inverse_norm = lax.rsqrt(norm_total + epsilon)
    all_queries = lax.all_gather(scaled, "ex", axis=0, tiled=True)
    own_scores = lax.psum_scatter(
        score_block(all_queries, train_grads), "co", scatter_dimension=0, tiled=True
    )
    normed = own_scores * inverse_norm[None, :]
    local_ids = example_ids - lax.axis_index("ex") * example_count
    return jnp.zeros_like(normed).at[:, local_ids].set(normed)


def solution(mesh):
    return jax.shard_map(
        shards,
        mesh=mesh,
        in_specs=(P("ex", "co"), P("ex", "co"), P(), P(), P("ex")),
        out_specs=P("co", "ex"),
        check_vma=False,
    )
```

profile of v0, /device:TPU:2, one launch (start us, length us, event | category | flops | bytes accessed | tf_op | source)
XLA Modules:
  0.0 214.1 jit_solution(3390543927937948465)
XLA Ops:
  6.5 0.0 all-gather.3.cloned.1.call-start
  6.6 0.9 select_reduce_fusion.1
  7.4 0.1 select_reduce_fusion
  7.5 1.9 broadcast_multiply_fusion
  9.4 0.0 all-gather.3.cloned.1.call-update
  9.5 0.0 reduce-scatter.2.cloned.1.call-start
  9.5 80.2 %all-gather.3.cloned.1.call-done = f32[1024,2048]{1,0:T(8,128)} async-done(((f32[64,2048]{1,0:T(8,128)}), f32[1024,2048]{1,0:T(8,128)}) %all-gather.3.cloned.1.call-update) | async-done | bytes 8388624 | tf_op jit(solution)/shard_map/all_gather | solution.py:43
  89.7 32.1 %fusion.5 = f32[1024,1024]{1,0:T(8,128)} fusion(f32[1024,2048]{1,0:T(8,128)} %all-gather.3.cloned.1.call-done, f32[1024,2048]{1,0:T(8,128)} %param.5), kind=kOutput, calls=%fused_computation.21 | convolution fusion | flops 25769803776 | bytes 20971520 | tf_op jit(solution)/shard_map/dot_general | solution.py:15
  121.8 0.0 copy-start
  121.8 0.0 reduce-scatter.2.cloned.1.call-update
  121.8 4.0 %multiply_reduce_fusion = f32[1024]{0:T(1024)S(1)} fusion(f32[1024,2048]{1,0:T(8,128)} %param.5), kind=kLoop, calls=%fused_computation.1 | loop fusion | flops 4193280 | bytes 8392704 | tf_op jit(solution)/shard_map/reduce_sum | solution.py:40
  125.8 33.2 %all-gather = f32[16384]{0:T(1024)S(1)} all-gather(f32[1024]{0:T(1024)S(1)} %multiply_reduce_fusion), channel_id=2, replica_groups=mesh['ex'=16,'co'=16] {'co'}, dimensions={0}, use_global_device_ids=true | all-gather | bytes 69632 | tf_op jit(solution)/shard_map/all_gather | solution.py:11
  159.1 0.0 copy-done
  159.1 42.9 %reduce-scatter.2.cloned.1.call-done = f32[64,1024]{1,0:T(8,128)} async-done(((f32[1024,1024]{1,0:T(8,128)}), f32[64,1024]{1,0:T(8,128)}) %reduce-scatter.2.cloned.1.call-update) | async-done | bytes 262160 | tf_op jit(solution)/shard_map/reduce_scatter | solution.py:44
  202.0 1.0 multiply_bitcast_fusion
  203.0 0.2 copy.10
  203.2 3.2 %scatter_custom_fusion = f32[64,1024]{0,1:T(8,128)S(1)} fusion(s32[1024]{0:T(1024)S(1)} %compare_select_fusion, f32[1024,64]{1,0:T(8,128)S(1)} %copy.10, f32[]{:T(128)} %constant.11.clone.1), kind=kCustom, calls=%fused_computation.4 | custom fusion | bytes 262148 | tf_op jit(solution)/shard_map/scatter | solution.py:49
  206.4 0.9 copy.11
  (5 shorter events, 0.1 us)
Async XLA Ops:
  6.5 83.1 %all-gather.3.cloned.1.call-start = ((), (), s32[]{:S(2)}) async-start(), calls=%async_computation.1 | async-start | bytes 8912896 | tf_op jit(solution)/shard_map/all_gather | solution.py:43
  9.5 192.5 %reduce-scatter.2.cloned.1.call-start = ((), (), s32[]{:S(2)}) async-start(), calls=%async_computation.2 | async-start | bytes 4456448 | tf_op jit(solution)/shard_map/reduce_scatter | solution.py:44
  121.8 37.3 %copy-start = (s32[1024]{0:T(1024)S(1)}, s32[1024]{0:T(1024)}, u32[]{:S(2)}) copy-start(s32[1024]{0:T(1024)} %param.9) | copy-start | bytes 12292
Sparse Core Ops, SparseCore 0:
  10.1 79.5 all-gather.2
  121.9 80.0 reduce-scatter.1
where the time goes:
time: 214 us
  waiting for transfers between devices  123 us (57%)
  blocking collectives  33.2 us (16%)
  matrix products  32.1 us (15%)
  between operations  13.5 us (6%)
  other arithmetic  7.89 us (4%)
  local copies, waits for them, and re-layouts  4.32 us (2%)
    all_gather x1, waiting for transfers between devices, shards(): all_queries = lax.all_gather(scaled, 'ex', axis=0, tiled=True)  80.2 us
    reduce_scatter x1, waiting for transfers between devices, shards(): lax.psum_scatter(score_block(all_queries, train_grads), 'co', scatter_dim...  42.9 us
    all_gather x1, blocking collectives, total_of_pieces(): return lax.all_gather(x, axis).sum(0)  33.2 us
    dot_general x1, matrix products, score_block(): lax.dot_general(query_rows, train_grads, (((1,), (1,)), ((), ())), precis...  32.1 us
  transfers between devices with their start and end apart: 2, of which 2 were waited for; matrix products, arithmetic and copies ran while one was open for 2% of the time, Pallas kernels for 0%

commit v1 on v0

--- a/solution.py
+++ b/solution.py
@@ -40,7 +40,9 @@
     squares = jnp.sum(train_grads * train_grads, axis=1)
     norm_total = total_of_pieces(squares, "co")
     inverse_norm = lax.rsqrt(norm_total + epsilon)
-    all_queries = lax.all_gather(scaled, "ex", axis=0, tiled=True)
+    all_queries = jnp.concatenate(
+        lax.all_to_all(jnp.stack([scaled] * lax.axis_size("ex")), "ex", 0, 0), axis=0
+    )
     own_scores = lax.psum_scatter(
         score_block(all_queries, train_grads), "co", scatter_dimension=0, tiled=True
     )

time: 214 us -> 233 us (1.089)
  blocking collectives: 33.2 us -> 136 us
  waiting for transfers between devices: 123 us -> 42.4 us
  matrix products: 32.1 us -> 27.7 us
    all_to_all x0 -> x1, blocking collectives: none -> 101 us  [shards(): lax.all_to_all(jnp.stack([scaled] * lax.axis_size('ex')), 'ex', 0, 0)]
    all_gather x1 -> x0, waiting for transfers between devices: 80.2 us -> none  [shards(): all_queries = lax.all_gather(scaled, 'ex', axis=0, tiled=True)]
    dot_general x1, matrix products: 32.1 us -> 27.7 us  [score_block(): lax.dot_general(query_rows, train_grads, (((1,), (1,)), ((), ())), precis...]
    all_gather x1, blocking collectives: 33.2 us -> 35.9 us  [total_of_pieces(): return lax.all_gather(x, axis).sum(0)]
  transfers between devices with their start and end apart: 2 -> 1, of which waited for: 2 -> 1; matrix products, arithmetic and copies ran while one was open for 2% -> 2% of each run, Pallas kernels for 0% -> 0%
where the time goes in v1:
time: 233 us; the launch traced here: 232 us
  blocking collectives  136 us (58%)
  waiting for transfers between devices  42.4 us (18%)
  matrix products  27.7 us (12%)
  between operations  13.5 us (6%)
  other arithmetic  7.05 us (3%)
  local copies, waits for them, and re-layouts  5.4 us (2%)
    all_to_all x1, blocking collectives, shards(): lax.all_to_all(jnp.stack([scaled] * lax.axis_size('ex')), 'ex', 0, 0)  101 us
    reduce_scatter x1, waiting for transfers between devices, shards(): lax.psum_scatter(score_block(all_queries, train_grads), 'co', scatter_dim...  42.4 us
    all_gather x1, blocking collectives, total_of_pieces(): return lax.all_gather(x, axis).sum(0)  35.9 us
    dot_general x1, matrix products, score_block(): lax.dot_general(query_rows, train_grads, (((1,), (1,)), ((), ())), precis...  27.7 us
  transfers between devices with their start and end apart: 1, of which 1 were waited for; matrix products, arithmetic and copies ran while one was open for 2% of the time, Pallas kernels for 0%

profile of v1, /device:TPU:2, one launch (start us, length us, event | category | flops | bytes accessed | tf_op | source)
XLA Modules:
  0.0 232.5 jit_solution(7067178665674551717)
XLA Ops:
  6.5 0.0 reduce-scatter.2.cloned.1.call-start
  6.6 0.9 select_reduce_fusion.1
  7.4 0.1 select_reduce_fusion
  7.5 1.1 broadcast_multiply_fusion
  8.6 0.0 slice-start
  8.6 1.1 stack.2
  9.7 0.0 slice-start.1
  9.7 100.5 %all_to_all.5 = f32[16,64,2048]{2,1,0:T(8,128)S(1)} all-to-all(f32[16,64,2048]{2,1,0:T(8,128)S(1)} %stack.2), channel_id=1, replica_groups=mesh['ex'=16,'co'=16] {'ex'}, dimensions={0} | all-to-all | bytes 16777216 | tf_op jit(solution)/shard_map/all_to_all | solution.py:44
  110.2 0.0 slice-done
  110.2 0.0 slice-done.1
  110.2 27.7 %fusion.5 = f32[1024,1024]{1,0:T(8,128)} fusion(f32[1024,2048]{1,0:T(8,128)S(1)} %bitcast.7, f32[1024,2048]{1,0:T(8,128)S(1)} %bitcast.6), kind=kOutput, calls=%fused_computation.21 | convolution fusion | flops 25769803776 | bytes 20971520 | tf_op jit(solution)/shard_map/dot_general | solution.py:15
  138.0 0.0 copy-start
  138.0 0.0 reduce-scatter.2.cloned.1.call-update
  138.0 4.0 %multiply_reduce_fusion = f32[1024]{0:T(1024)S(1)} fusion(f32[1024,2048]{1,0:T(8,128)} %param.5), kind=kLoop, calls=%fused_computation.1 | loop fusion | flops 4193280 | bytes 8392704 | tf_op jit(solution)/shard_map/reduce_sum | solution.py:40
  142.0 35.9 %all-gather = f32[16384]{0:T(1024)S(1)} all-gather(f32[1024]{0:T(1024)S(1)} %multiply_reduce_fusion), channel_id=2, replica_groups=mesh['ex'=16,'co'=16] {'co'}, dimensions={0}, use_global_device_ids=true | all-gather | bytes 69632 | tf_op jit(solution)/shard_map/all_gather | solution.py:11
  177.9 0.0 copy-done
  177.9 42.4 %reduce-scatter.2.cloned.1.call-done = f32[64,1024]{1,0:T(8,128)} async-done(((f32[1024,1024]{1,0:T(8,128)}), f32[64,1024]{1,0:T(8,128)}) %reduce-scatter.2.cloned.1.call-update) | async-done | bytes 262160 | tf_op jit(solution)/shard_map/reduce_scatter | solution.py:46
  220.4 1.0 multiply_bitcast_fusion
  221.3 0.2 copy.10
  221.5 3.2 %scatter_custom_fusion = f32[64,1024]{0,1:T(8,128)S(1)} fusion(s32[1024]{0:T(1024)S(1)} %compare_select_fusion, f32[1024,64]{1,0:T(8,128)S(1)} %copy.10, f32[]{:T(128)} %constant.11.clone.1), kind=kCustom, calls=%fused_computation.4 | custom fusion | bytes 262148 | tf_op jit(solution)/shard_map/scatter | solution.py:51
  224.8 0.9 copy.11
  (6 shorter events, 0.1 us)
Async XLA Ops:
  6.5 213.8 %reduce-scatter.2.cloned.1.call-start = ((), (), s32[]{:S(2)}) async-start(), calls=%async_computation.2 | async-start | bytes 4456448 | tf_op jit(solution)/shard_map/reduce_scatter | solution.py:46
  8.6 101.6 %slice-start = ((s8[8388608]{0:T(1024)(128)(4,1)}), s8[4194304]{0:T(1024)(128)(4,1)S(1)}, s32[]{:S(2)}) async-start(s8[8388608]{0:T(1024)(128)(4,1)} %bitcast.5), calls=%async_computation.3 | async-start | bytes 8388608
  9.7 100.6 %slice-start.1 = ((s8[8388608]{0:T(1024)(128)(4,1)}), s8[4194304]{0:T(1024)(128)(4,1)S(1)}, s32[]{:S(2)}) async-start(s8[8388608]{0:T(1024)(128)(4,1)} %bitcast.5), calls=%async_computation.4 | async-start | bytes 8388608
  138.0 39.9 %copy-start = (s32[1024]{0:T(1024)S(1)}, s32[1024]{0:T(1024)}, u32[]{:S(2)}) copy-start(s32[1024]{0:T(1024)} %param.9) | copy-start | bytes 12292
Sparse Core Ops, SparseCore 0:
  138.1 82.1 reduce-scatter.1
